TPU v7x, 32 devices: a whole 2x2x4 slice. The times are simulated.
32 devices in a mesh: replica: 16 (over z, y, core), fsdp: 2 (over x).
Axes of the slice: x: 2, y: 2, z: 4, core: 2. Of those that a mesh axis runs over, the one named last changes fastest.
Arguments:
- inner_weights: float32 [16, 3, 24, 6144], P('replica', None, None, 'fsdp'), may hold values from -8 to 8
- anchor: float32 [3, 24, 6144], P(None, None, 'fsdp'), may hold values from -4 to 4
- outer_moment: float32 [3, 24, 6144], P(None, None, 'fsdp'), may hold values from -3 to 3
- adam_first: float32 [16, 3, 24, 6144], P('replica', None, None, 'fsdp'), may hold values from -2 to 2
- adam_second: float32 [16, 3, 24, 6144], P('replica', None, None, 'fsdp'), may hold values from 0.1 to 1
- grad_parts: bfloat16 [16, 2, 3, 24, 6144], P('replica', 'fsdp'), may hold values from -2.5 to 2.5
Outputs:
- fresh_weights: bfloat16 [3, 24, 6144], replicated
- anchor_new: float32 [3, 24, 6144], P(None, None, 'fsdp')
- moment_new: float32 [3, 24, 6144], P(None, None, 'fsdp')
- first_new: float32 [16, 3, 24, 6144], P('replica', None, None, 'fsdp')
- second_new: float32 [16, 3, 24, 6144], P('replica', None, None, 'fsdp')
All inputs are finite; a program needn't handle non-finite values.
Results may differ from a plain program's by a relative error of at most 0.0025.
Values may be sent and summed in bfloat16 or wider, within the bound.
A program may use at most 64 MiB of HBM per device.

v0:
```python
import jax
import jax.numpy as jnp
from jax import lax
from jax.sharding import PartitionSpec as P

beta_one = 0.9
beta_two = 0.95
correct_one = 0.99997343860111
correct_two = 0.994079470779666
adam_eps = 1e-08
inner_rate = 0.1
decay_rate = 0.1
outer_rate = 0.7
outer_mu = 0.9


def inner_update(weights, anchor_now, first_now, second_now, gradient):
    first_new = beta_one * first_now + (1.0 - beta_one) * gradient
    second_new = beta_two * second_now + (1.0 - beta_two) * gradient * gradient
    update = first_new / correct_one / (jnp.sqrt(second_new / correct_two) + adam_eps)
    stepped = weights - inner_rate * (update + decay_rate * weights)
    return (first_new, second_new, anchor_now - stepped)


def outer_update(mean_delta, moment_now, anchor_now):
    moment_new = outer_mu * moment_now + mean_delta
    anchor_new = anchor_now - outer_rate * (mean_delta + outer_mu * moment_new)
    return (moment_new, anchor_new)


def per_device(inner_weights, anchor, outer_moment, adam_first, adam_second, grad_parts):
    received = lax.all_to_all(grad_parts, "fsdp", split_axis=4, concat_axis=1, tiled=True)
    gradient = jnp.sum(received.astype(jnp.float32), axis=1)
    first_new, second_new, pseudo = inner_update(
        inner_weights, anchor[None], adam_first, adam_second, gradient
    )
    pseudo = pseudo[0]
    workers = lax.axis_size("replica")
    summed = lax.psum(pseudo, "replica")
    moment_new, anchor_new = outer_update(summed / workers, outer_moment, anchor)
    fresh_weights = lax.all_gather(anchor_new.astype(jnp.bfloat16), "fsdp", axis=2, tiled=True)
    return (fresh_weights, anchor_new, moment_new, first_new, second_new)


def solution(mesh):
    in_specs = (
        P("replica", None, None, "fsdp"),
        P(None, None, "fsdp"),
        P(None, None, "fsdp"),
        P("replica", None, None, "fsdp"),
        P("replica", None, None, "fsdp"),
        P("replica", "fsdp", None, None, None),
    )
    out_specs = (
        P(),
        P(None, None, "fsdp"),
        P(None, None, "fsdp"),
        P("replica", None, None, "fsdp"),
        P("replica", None, None, "fsdp"),
    )
    return jax.shard_map(
        per_device, mesh=mesh, in_specs=in_specs, out_specs=out_specs, check_vma=False
    )
```

profile of v0, /device:TPU:0, one launch (start us, length us, event | category | flops | bytes accessed | tf_op | source)
XLA Modules:
  0.0 183.9 jit_solution(3862538814976636377)
XLA Ops:
  7.2 0.0 all-reduce.2.cloned.1.call-start
  7.2 8.0 %copy.50 = bf16[1,1,3,24,6144]{3,2,1,0,4:T(4,128)(2,1)} copy(bf16[1,1,3,24,6144]{4,3,2,1,0:T(8,128)(2,1)} %param.11) | data formatting | bytes 1769472 | tf_op args[5]
  15.3 8.1 %reshape.49 = bf16[2,2,110592]{2,1,0:T(2,128)(2,1)S(1)} reshape(bf16[6144,1,1,3,24]{4,3,2,1,0:T(4,128)(2,1)} %bitcast.18) | data formatting | bytes 1769472
  23.4 15.9 %all_to_all.4 = bf16[2,2,110592]{2,1,0:T(2,128)(2,1)S(1)} all-to-all(bf16[2,2,110592]{2,1,0:T(2,128)(2,1)S(1)} %reshape.49), channel_id=1, replica_groups=mesh['replica'=16,'fsdp'=2] {'fsdp'}, dimensions={0} | all-to-all | bytes 1769472 | tf_op jit(solution)/shard_map/all_to_all | solution.py:32
  39.3 8.9 %reshape.50 = bf16[6144,1,1,3,24]{4,3,2,1,0:T(4,128)(2,1)} reshape(bf16[2,2,110592]{2,1,0:T(2,128)(2,1)S(1)} %all_to_all.4) | data formatting | bytes 1769472
  48.1 11.1 %convert_reduce_fusion = f32[3,24,3072]{1,0,2:T(4,128)} fusion(bf16[3,24,2,3072]{1,0,3,2:T(4,128)(2,1)} %bitcast.17), kind=kLoop, calls=%fused_computation | loop fusion | flops 663552 | bytes 1769472 | tf_op jit(solution)/shard_map/reduce_sum | solution.py:33
  59.2 0.0 copy-start
  59.2 0.0 copy-start.1
  59.2 0.0 copy-start.2
  59.2 5.1 %copy.51 = f32[3,24,3072]{2,1,0:T(8,128)S(1)} copy(f32[3,24,3072]{1,0,2:T(4,128)} %convert_reduce_fusion) | data formatting | bytes 1769472 | tf_op jit(solution)/shard_map/reduce_sum | solution.py:33
  64.3 0.0 copy-done
  64.3 0.0 copy-done.1
  64.4 0.0 copy-done.2
  64.4 3.1 %fusion.2 = (f32[3,24,3072]{2,1,0:T(8,128)}, f32[1,3,24,3072]{3,2,1,0:T(8,128)}, f32[1,3,24,3072]{3,2,1,0:T(8,128)}) fusion(f32[3,24,3072]{2,1,0:T(8,128)S(1)} %copy-done, f32[1,3,24,3072]{3,2,1,0:T(8,128)S(1)} %copy-done.1, f32[3,24,3072]{2,1,0:T(8,128)S(1)} %copy.51, f32[1,3,24,3072]{3,2,1,0:T(8,128)S(1)} %copy-done.2, f32[1,3,24,3072]{3,2,1,0:T(8,128)} %param.10), kind=kLoop, calls=%fused_computation.6 | loop fusion | flops 3538944 | bytes 7077888 | tf_op jit(solution)/shard_map/squeeze | solution.py:37
  67.5 0.0 all-reduce.2.cloned.1.call-update
  67.5 94.0 %all-reduce.2.cloned.1.call-done = f32[3,24,3072]{2,1,0:T(8,128)} async-done(((f32[3,24,3072]{2,1,0:T(8,128)}), f32[3,24,3072]{2,1,0:T(8,128)}) %all-reduce.2.cloned.1.call-update) | async-done | bytes 884752 | tf_op jit(solution)/shard_map/psum | solution.py:39
  161.5 2.9 %fusion.3 = (bf16[3,24,3072]{2,1,0:T(8,128)(2,1)S(1)}, f32[3,24,3072]{2,1,0:T(8,128)}, f32[3,24,3072]{2,1,0:T(8,128)}) fusion(f32[3,24,3072]{2,1,0:T(8,128)S(1)} %copy-done, f32[3,24,3072]{2,1,0:T(8,128)} %all-reduce.2.cloned.1.call-done, f32[3,24,3072]{2,1,0:T(8,128)} %param.8), kind=kLoop, calls=%fused_computation.9 | loop fusion | flops 1769472 | bytes 4866048 | tf_op jit(solution)/shard_map/convert_element_type | solution.py:41
  164.4 11.7 %all_gather.3 = bf16[3,24,6144]{2,1,0:T(8,128)(2,1)S(1)} all-gather(bf16[3,24,3072]{2,1,0:T(8,128)(2,1)S(1)} %get-tuple-element.15), channel_id=1, replica_groups=mesh['replica'=16,'fsdp'=2] {'fsdp'}, dimensions={2}, use_global_device_ids=true | all-gather | bytes 1327104 | tf_op jit(solution)/shard_map/all_gather | solution.py:41
  176.1 0.9 copy.54
Async XLA Ops:
  7.2 154.3 %all-reduce.2.cloned.1.call-start = ((), (), s32[]{:S(2)}) async-start(), calls=%async_computation.1 | async-start | bytes 1769472 | tf_op jit(solution)/shard_map/psum | solution.py:39
  59.2 5.1 %copy-start = (f32[3,24,3072]{2,1,0:T(8,128)S(1)}, f32[3,24,3072]{2,1,0:T(8,128)}, u32[]{:S(2)}) copy-start(f32[3,24,3072]{2,1,0:T(8,128)} %param.7) | copy-start | bytes 2654212
  59.2 5.1 %copy-start.1 = (f32[1,3,24,3072]{3,2,1,0:T(8,128)S(1)}, f32[1,3,24,3072]{3,2,1,0:T(8,128)}, u32[]{:S(2)}) copy-start(f32[1,3,24,3072]{3,2,1,0:T(8,128)} %param.6) | copy-start | bytes 2654212
  59.2 5.1 %copy-start.2 = (f32[1,3,24,3072]{3,2,1,0:T(8,128)S(1)}, f32[1,3,24,3072]{3,2,1,0:T(8,128)}, u32[]{:S(2)}) copy-start(f32[1,3,24,3072]{3,2,1,0:T(8,128)} %param.9) | copy-start | bytes 2654212
Sparse Core Ops, SparseCore 0:
  67.6 93.8 all-reduce.1
where the time goes:
time: 185 us; the launch traced here: 184 us
  waiting for transfers between devices  94 us (51%)
  local copies, waits for them, and re-layouts  31.1 us (17%)
  blocking collectives  27.6 us (15%)
  other arithmetic  17.1 us (9%)
  between operations  14.1 us (8%)
    psum x1, waiting for transfers between devices, per_device(): summed = lax.psum(pseudo, 'replica')  94 us
    unnamed x10, local copies, waits for them, and re-layouts  26 us
    all_to_all x1, blocking collectives, per_device(): lax.all_to_all(grad_parts, 'fsdp', split_axis=4, concat_axis=1, tiled=True)  15.9 us
    all_gather x1, blocking collectives, per_device(): lax.all_gather(anchor_new.astype(jnp.bfloat16), 'fsdp', axis=2, tiled=True)  11.7 us
    reduce_sum x1, other arithmetic, per_device(): gradient = jnp.sum(received.astype(jnp.float32), axis=1)  11.1 us
    reduce_sum x1, local copies, waits for them, and re-layouts, per_device(): gradient = jnp.sum(received.astype(jnp.float32), axis=1)  5.09 us
  transfers between devices with their start and end apart: 1, of which 1 were waited for; matrix products, arithmetic and copies ran while one was open for 0% of the time, Pallas kernels for 0%

commit v1 on v0

--- a/solution.py
+++ b/solution.py
@@ -1,7 +1,15 @@
+import functools
+
 import jax
 import jax.numpy as jnp
 from jax import lax
+from jax.experimental import pallas as pl
+from jax.experimental.pallas import tpu as pltpu
 from jax.sharding import PartitionSpec as P
+
+MESH = pl.DeviceIdType.MESH
+LANE = 128
+SKEW = 2
 
 beta_one = 0.9
 beta_two = 0.95
@@ -28,21 +36,270 @@
     return (moment_new, anchor_new)
 
 
-def per_device(inner_weights, anchor, outer_moment, adam_first, adam_second, grad_parts):
-    received = lax.all_to_all(grad_parts, "fsdp", split_axis=4, concat_axis=1, tiled=True)
-    gradient = jnp.sum(received.astype(jnp.float32), axis=1)
-    first_new, second_new, pseudo = inner_update(
-        inner_weights, anchor[None], adam_first, adam_second, gradient
-    )
-    pseudo = pseudo[0]
-    workers = lax.axis_size("replica")
-    summed = lax.psum(pseudo, "replica")
-    moment_new, anchor_new = outer_update(summed / workers, outer_moment, anchor)
-    fresh_weights = lax.all_gather(anchor_new.astype(jnp.bfloat16), "fsdp", axis=2, tiled=True)
-    return (fresh_weights, anchor_new, moment_new, first_new, second_new)
+def plan(cols, workers):
+    tiles = cols // LANE
+    pipes = tiles
+    while pipes % 2 == 0:
+        pipes //= 2
+    width = cols // pipes
+    steps = workers.bit_length() - 1
+    halvings, size = 0, width
+    while halvings < steps and size % (2 * LANE) == 0:
+        size //= 2
+        halvings += 1
+    return pipes, width, halvings, steps
+
+
+def kernel(n, workers, pipes, width, halvings, steps, *refs):
+    (w_h, a_h, m_h, f_h, s_h, g_h, fresh_o, anchor_o, moment_o, first_o, second_o) = refs[:11]
+    (w_v, a_v, m_v, f_v, s_v, g_v, g_r, first_v, second_v, acc, tot, anew, mnew, fresh) = refs[11:25]
+    (in_sem, out_sem, gs, gr, rs, rr, ags, agr, fs, fr, ws, wr) = refs[25:37]
+    parts = refs[37:]
+    cols = w_v.shape[-1]
+    me = lax.axis_index("replica")
+    mine = lax.axis_index("fsdp")
+
+    def bit_of(b):
+        return (me // 2**b) % 2
+
+    def partner(b):
+        return me + 2**b * (1 - 2 * bit_of(b))
+
+    def at(ref, off, size):
+        return ref.at[:, :, pl.ds(pl.multiple_of(off, LANE), size)]
+
+    loads, grads = [], []
+    for q in range(pipes):
+        row = []
+        for i, (src, dst) in enumerate(
+            ((f_h, f_v), (s_h, s_v), (w_h, w_v), (a_h, a_v), (m_h, m_v))
+        ):
+            row.append(pltpu.make_async_copy(at(src, q * width, width), at(dst, q * width, width), in_sem.at[q, i]))
+        row.append(
+            pltpu.make_async_copy(at(g_h, mine * cols + q * width, width), at(g_v, q * width, width), in_sem.at[q, 5])
+        )
+        loads.append(row)
+        row = []
+        for s in range(1, n):
+            peer = lax.rem(mine + s, n)
+            row.append(
+                pltpu.make_async_remote_copy(
+                    src_ref=at(g_h, peer * cols + q * width, width),
+                    dst_ref=at(g_r.at[s - 1], q * width, width),
+                    send_sem=gs.at[q, s - 1],
+                    recv_sem=gr.at[q, s - 1],
+                    device_id={"fsdp": peer},
+                    device_id_type=MESH,
+                )
+            )
+        grads.append(row)
+
+    barrier = pltpu.get_barrier_semaphore()
+    for s in range(1, n):
+        pl.semaphore_signal(barrier, inc=1, device_id={"fsdp": lax.rem(mine + s, n)}, device_id_type=MESH)
+    for b in range(steps):
+        pl.semaphore_signal(barrier, inc=1, device_id={"replica": partner(b)}, device_id_type=MESH)
+    for row in loads:
+        for copy in row:
+            copy.start()
+    pl.semaphore_wait(barrier, n - 1 + steps)
+    for row in grads:
+        for copy in row:
+            copy.start()
+
+    sent, stores = [], []
+
+    def store(src, dst, q, i):
+        copy = pltpu.make_async_copy(src, dst, out_sem.at[q, i])
+        copy.start()
+        stores.append(copy)
+
+    def outer(off, size):
+        @pl.loop(0, size // LANE)
+        def _(j):
+            c = pl.ds(pl.multiple_of(off + j * LANE, LANE), LANE)
+            moment_new, anchor_new = outer_update(tot[:, :, c] / workers, m_v[:, :, c], a_v[:, :, c])
+            mnew[:, :, c] = moment_new
+            anew[:, :, c] = anchor_new
+            d = pl.ds(pl.multiple_of(mine * cols + off + j * LANE, LANE), LANE)
+            fresh[:, :, d] = anchor_new.astype(fresh.dtype)
+
+    def pipe(q):
+        base = q * width
+        for copy in loads[q]:
+            copy.wait()
+        for copy in grads[q]:
+            copy.wait_recv()
+            sent.append(copy)
+
+        @pl.loop(0, width // LANE)
+        def _(j):
+            c = pl.ds(pl.multiple_of(base + j * LANE, LANE), LANE)
+            gradient = g_v[:, :, c].astype(jnp.float32)
+            for s in range(n - 1):
+                gradient = gradient + g_r[s, :, :, c].astype(jnp.float32)
+            first_new, second_new, pseudo = inner_update(
+                w_v[:, :, c], a_v[:, :, c], f_v[:, :, c], s_v[:, :, c], gradient
+            )
+            first_v[:, :, c] = first_new
+            second_v[:, :, c] = second_new
+            acc[:, :, c] = pseudo
+
+        store(at(first_v, base, width), at(first_o, base, width), q, 0)
+        store(at(second_v, base, width), at(second_o, base, width), q, 1)
+
+        off, size = base, width
+        offs = [off]
+        for b in range(steps):
+            if b < halvings:
+                size //= 2
+                give = off + (1 - bit_of(b)) * size
+                off = off + bit_of(b) * size
+                offs.append(off)
+            else:
+                give = off
+            copy = pltpu.make_async_remote_copy(
+                src_ref=at(acc, give, size),
+                dst_ref=at(parts[b], q * size, size),
+                send_sem=rs.at[q, b],
+                recv_sem=rr.at[q, b],
+                device_id={"replica": partner(b)},
+                device_id_type=MESH,
+            )
+            copy.start()
+            yield
+            if b < halvings:
+                copy.wait_recv()
+                sent.append(copy)
+            else:
+                copy.wait()
+            into = tot if b == steps - 1 else acc
+
+            @pl.loop(0, size // LANE)
+            def _(j, b=b, off=off, size=size, into=into):
+                c = pl.ds(pl.multiple_of(off + j * LANE, LANE), LANE)
+                d = pl.ds(pl.multiple_of(q * size + j * LANE, LANE), LANE)
+                into[:, :, c] = acc[:, :, c] + parts[b][:, :, d]
+
+        for b in reversed(range(halvings)):
+            copy = pltpu.make_async_remote_copy(
+                src_ref=at(tot, off, size),
+                dst_ref=at(tot, off, size),
+                send_sem=ags.at[q, b],
+                recv_sem=agr.at[q, b],
+                device_id={"replica": partner(b)},
+                device_id_type=MESH,
+            )
+            copy.start()
+            sent.append(copy)
+            if b == 0:
+                outer(off, size)
+                fresh_out = []
+                for s in range(1, n):
+                    out = pltpu.make_async_remote_copy(
+                        src_ref=at(fresh, mine * cols + off, size),
+                        dst_ref=at(fresh, mine * cols + off, size),
+                        send_sem=fs.at[q, s - 1],
+                        recv_sem=fr.at[q, s - 1],
+                        device_id={"fsdp": lax.rem(mine + s, n)},
+                        device_id_type=MESH,
+                    )
+                    out.start()
+                    sent.append(out)
+                    fresh_out.append(out)
+                half_off, half = off, size
+            yield
+            copy.wait_recv()
+            off = offs[b]
+            size *= 2
+        outer(base + (1 - bit_of(0)) * half, half)
+        store(at(mnew, base, width), at(moment_o, base, width), q, 2)
+        store(at(anew, base, width), at(anchor_o, base, width), q, 3)
+        store(at(fresh, mine * cols + base, width), at(fresh_o, mine * cols + base, width), q, 4)
+        yield
+        passed = []
+        for s in range(1, n):
+            fresh_out[s - 1].wait_recv()
+            place = lax.rem(mine + n - s, n) * cols + half_off
+            copy = pltpu.make_async_remote_copy(
+                src_ref=at(fresh, place, half),
+                dst_ref=at(fresh, place, half),
+                send_sem=ws.at[q, s - 1],
+                recv_sem=wr.at[q, s - 1],
+                device_id={"replica": partner(0)},
+                device_id_type=MESH,
+            )
+            copy.start()
+            sent.append(copy)
+            passed.append(copy)
+        yield
+        for s in range(1, n):
+            passed[s - 1].wait_recv()
+            place = lax.rem(mine + n - s, n) * cols + base
+            store(at(fresh, place, width), at(fresh_o, place, width), q, 4 + s)
+
+    live = [pipe(q) for q in range(pipes)]
+    turn = 0
+    while any(p is not None for p in live):
+        for q in range(pipes):
+            if live[q] is not None and turn >= q * SKEW:
+                try:
+                    next(live[q])
+                except StopIteration:
+                    live[q] = None
+        turn += 1
+    for copy in sent:
+        copy.wait_send()
+    for copy in stores:
+        copy.wait()
 
 
 def solution(mesh):
+    n, workers = mesh.shape["fsdp"], mesh.shape["replica"]
+
+    def per_device(inner_weights, anchor, outer_moment, adam_first, adam_second, grad_parts):
+        layers, rows, cols = anchor.shape
+        pipes, width, halvings, steps = plan(cols, workers)
+        shard, whole = (layers, rows, cols), (layers, rows, n * cols)
+        f32, bf16 = jnp.float32, jnp.bfloat16
+        parts = [
+            pltpu.VMEM((layers, rows, pipes * (width >> min(b + 1, halvings))), f32) for b in range(steps)
+        ]
+        dma = pltpu.SemaphoreType.DMA
+        fresh_weights, anchor_new, moment_new, first_new, second_new = pl.pallas_call(
+            functools.partial(kernel, n, workers, pipes, width, halvings, steps),
+            out_shape=(
+                jax.ShapeDtypeStruct(whole, bf16),
+                jax.ShapeDtypeStruct(shard, f32),
+                jax.ShapeDtypeStruct(shard, f32),
+                jax.ShapeDtypeStruct(shard, f32),
+                jax.ShapeDtypeStruct(shard, f32),
+            ),
+            in_specs=[pl.BlockSpec(memory_space=pl.ANY)] * 6,
+            out_specs=[pl.BlockSpec(memory_space=pl.ANY)] * 5,
+            scratch_shapes=[pltpu.VMEM(shard, f32)] * 5
+            + [pltpu.VMEM(shard, bf16), pltpu.VMEM((n - 1,) + shard, bf16)]
+            + [pltpu.VMEM(shard, f32)] * 6
+            + [pltpu.VMEM(whole, bf16)]
+            + [
+                dma((pipes, 6)),
+                dma((pipes, 4 + n)),
+                dma((pipes, n - 1)),
+                dma((pipes, n - 1)),
+                dma((pipes, steps)),
+                dma((pipes, steps)),
+                dma((pipes, halvings)),
+                dma((pipes, halvings)),
+                dma((pipes, n - 1)),
+                dma((pipes, n - 1)),
+                dma((pipes, n - 1)),
+                dma((pipes, n - 1)),
+            ]
+            + parts,
+            compiler_params=pltpu.CompilerParams(collective_id=0, has_side_effects=True),
+        )(inner_weights[0], anchor, outer_moment, adam_first[0], adam_second[0], grad_parts[0, 0])
+        return (fresh_weights, anchor_new, moment_new, first_new[None], second_new[None])
+
     in_specs = (
         P("replica", None, None, "fsdp"),
         P(None, None, "fsdp"),

time: 185 us -> 55.1 us (0.30)
  waiting for transfers between devices: 94 us -> 0 us
  Pallas kernels: 0 us -> 46.1 us
  blocking collectives: 27.6 us -> 0 us
  local copies, waits for them, and re-layouts: 31.1 us -> 7.59 us
  other arithmetic: 17.1 us -> 0 us
  between operations: 14.1 us -> 0.65 us
    psum x1 -> x0, waiting for transfers between devices: 94 us -> none  [per_device(): summed = lax.psum(pseudo, 'replica')]
    pallas_call x0 -> x1, Pallas kernels: none -> 46.1 us  [per_device(): pl.pallas_call(functools.partial(kernel, n, workers, pipes, width, halvin...]
    unnamed x10 -> x13, local copies, waits for them, and re-layouts: 26 us -> 7.59 us
    all_to_all x1 -> x0, blocking collectives: 15.9 us -> none  [per_device(): lax.all_to_all(grad_parts, 'fsdp', split_axis=4, concat_axis=1, tiled=True)]
    all_gather x1 -> x0, blocking collectives: 11.7 us -> none  [per_device(): lax.all_gather(anchor_new.astype(jnp.bfloat16), 'fsdp', axis=2, tiled=True)]
    reduce_sum x1 -> x0, other arithmetic: 11.1 us -> none  [per_device(): gradient = jnp.sum(received.astype(jnp.float32), axis=1)]
    reduce_sum x1 -> x0, local copies, waits for them, and re-layouts: 5.09 us -> none  [per_device(): gradient = jnp.sum(received.astype(jnp.float32), axis=1)]
    squeeze x1 -> x0, other arithmetic: 3.11 us -> none  [per_device(): pseudo = pseudo[0]]
  transfers between devices with their start and end apart: 1 -> 0, of which waited for: 1 -> 0; matrix products, arithmetic and copies ran while one was open for 0% -> 0% of each run, Pallas kernels for 0% -> 0%
where the time goes in v1:
time: 55.1 us; the launch traced here: 54.3 us
  Pallas kernels  46.1 us (84%)
  local copies, waits for them, and re-layouts  7.59 us (14%)
  between operations  0.65 us (1%)
    pallas_call x1, Pallas kernels, per_device(): pl.pallas_call(functools.partial(kernel, n, workers, pipes, width, halvin...  46.1 us
    unnamed x13, local copies, waits for them, and re-layouts  7.59 us

profile of v1, /device:TPU:0, one launch (start us, length us, event | category | flops | bytes accessed | tf_op | source)
XLA Modules:
  0.0 54.3 jit_solution(14613014884375449376)
XLA Ops:
  0.6 46.1 %shard_map.101 = (bf16[3,24,6144]{2,1,0:T(8,128)(2,1)}, f32[3,24,3072]{2,1,0:T(8,128)}, f32[3,24,3072]{2,1,0:T(8,128)}, f32[3,24,3072]{2,1,0:T(8,128)}, f32[3,24,3072]{2,1,0:T(8,128)}) custom-call(f32[3,24,3072]{2,1,0:T(8,128)} %bitcast.8, f32[3,24,3072]{2,1,0:T(8,128)} %refs_1_.1, f32[3,24,3072]{2,1,0:T(8,128)} %refs_2_.1, f32[3,24,3072]{2,1,0:T(8,128)} %bitcast.9, ...), custom_call_target="tpu_custom_call" | custom-call | tf_op jit(solution)/shard_map/pallas_call | solution.py:269
  46.7 0.0 copy-start.3
  46.8 2.2 %copy.16 = bf16[3,24,6144]{2,1,0:T(8,128)(2,1)} copy(bf16[3,24,6144]{2,1,0:T(8,128)(2,1)} %get-tuple-element.20) | data formatting | bytes 1769472
  49.0 0.0 copy-done.3
  49.0 0.0 copy-start.2
  49.0 0.9 %copy.17 = f32[3,24,3072]{2,1,0:T(8,128)} copy(f32[3,24,3072]{2,1,0:T(8,128)S(1)} %copy-done.3) | data formatting | bytes 1769472
  49.9 0.6 %copy-done.2 = f32[3,24,3072]{2,1,0:T(8,128)S(1)} copy-done((f32[3,24,3072]{2,1,0:T(8,128)S(1)}, f32[3,24,3072]{2,1,0:T(8,128)}, u32[]{:S(2)}) %copy-start.2) | copy-done | bytes 884760
  50.5 0.0 copy-start.1
  50.5 0.9 %copy.18 = f32[3,24,3072]{2,1,0:T(8,128)} copy(f32[3,24,3072]{2,1,0:T(8,128)S(1)} %copy-done.2) | data formatting | bytes 1769472
  51.4 0.6 %copy-done.1 = f32[3,24,3072]{2,1,0:T(8,128)S(1)} copy-done((f32[3,24,3072]{2,1,0:T(8,128)S(1)}, f32[3,24,3072]{2,1,0:T(8,128)}, u32[]{:S(2)}) %copy-start.1) | copy-done | bytes 884760
  51.9 0.0 copy-start
  51.9 0.9 %copy.19 = f32[1,3,24,3072]{3,2,1,0:T(8,128)} copy(f32[1,3,24,3072]{3,2,1,0:T(8,128)S(1)} %bitcast.7) | data formatting | bytes 1769472
  52.9 0.6 %copy-done = f32[3,24,3072]{2,1,0:T(8,128)S(1)} copy-done((f32[3,24,3072]{2,1,0:T(8,128)S(1)}, f32[3,24,3072]{2,1,0:T(8,128)}, u32[]{:S(2)}) %copy-start) | copy-done | bytes 884760
  53.4 0.9 %copy.20 = f32[1,3,24,3072]{3,2,1,0:T(8,128)} copy(f32[1,3,24,3072]{3,2,1,0:T(8,128)S(1)} %bitcast.6) | data formatting | bytes 1769472
Async XLA Ops:
  46.7 2.2 %copy-start.3 = (f32[3,24,3072]{2,1,0:T(8,128)S(1)}, f32[3,24,3072]{2,1,0:T(8,128)}, u32[]{:S(2)}) copy-start(f32[3,24,3072]{2,1,0:T(8,128)} %get-tuple-element.21) | copy-start | bytes 2654212
  49.0 1.5 %copy-start.2 = (f32[3,24,3072]{2,1,0:T(8,128)S(1)}, f32[3,24,3072]{2,1,0:T(8,128)}, u32[]{:S(2)}) copy-start(f32[3,24,3072]{2,1,0:T(8,128)} %get-tuple-element.22) | copy-start | bytes 2654212
  50.5 1.5 %copy-start.1 = (f32[3,24,3072]{2,1,0:T(8,128)S(1)}, f32[3,24,3072]{2,1,0:T(8,128)}, u32[]{:S(2)}) copy-start(f32[3,24,3072]{2,1,0:T(8,128)} %get-tuple-element.13) | copy-start | bytes 2654212
  51.9 1.5 %copy-start = (f32[3,24,3072]{2,1,0:T(8,128)S(1)}, f32[3,24,3072]{2,1,0:T(8,128)}, u32[]{:S(2)}) copy-start(f32[3,24,3072]{2,1,0:T(8,128)} %get-tuple-element.14) | copy-start | bytes 2654212

commit v2 on v1

v2 whole, which is shorter than its diff:
```python
import functools

import jax
import jax.numpy as jnp
from jax import lax
from jax.experimental import pallas as pl
from jax.experimental.pallas import tpu as pltpu
from jax.sharding import PartitionSpec as P

MESH = pl.DeviceIdType.MESH
LANE = 128
CHUNK = 512
SKEW = 0

beta_one = 0.9
beta_two = 0.95
correct_one = 0.99997343860111
correct_two = 0.994079470779666
adam_eps = 1e-08
inner_rate = 0.1
decay_rate = 0.1
outer_rate = 0.7
outer_mu = 0.9


def inner_update(weights, anchor_now, first_now, second_now, gradient):
    first_new = beta_one * first_now + (1.0 - beta_one) * gradient
    second_new = beta_two * second_now + (1.0 - beta_two) * gradient * gradient
    update = first_new / (jnp.sqrt(second_new) * (correct_one / correct_two**0.5) + correct_one * adam_eps)
    stepped = weights - inner_rate * (update + decay_rate * weights)
    return (first_new, second_new, anchor_now - stepped)


def outer_update(mean_delta, moment_now, anchor_now):
    moment_new = outer_mu * moment_now + mean_delta
    anchor_new = anchor_now - outer_rate * (mean_delta + outer_mu * moment_new)
    return (moment_new, anchor_new)


def plan(cols, workers):
    tiles = cols // LANE
    pipes = tiles
    while pipes % 2 == 0:
        pipes //= 2
    width = cols // pipes
    steps = workers.bit_length() - 1
    halvings, size = 0, width
    while halvings < steps and size % (2 * LANE) == 0:
        size //= 2
        halvings += 1
    return pipes, width, halvings, steps


def sweep(size, body):
    step = size
    while step > CHUNK:
        step //= 2
    if step == size:
        body(0, size)
    else:

        @pl.loop(0, size // step)
        def _(j):
            body(j * step, step)


def kernel(n, workers, pipes, width, halvings, steps, *refs):
    (w_h, a_h, m_h, f_h, s_h, g_h, fresh_o, anchor_o, moment_o, first_o, second_o) = refs[:11]
    (w_v, a_v, m_v, f_v, s_v, g_v, g_r, acc, tot, fresh) = refs[11:21]
    (in_sem, out_sem, gs, gr, rs, rr, ags, agr, fs, fr, ws, wr) = refs[21:33]
    parts = refs[33:]
    layers, _, cols = w_v.shape
    groups, pipes = pipes, layers * pipes
    me = lax.axis_index("replica")
    mine = lax.axis_index("fsdp")

    def bit_of(b):
        return (me // 2**b) % 2

    def partner(b):
        return me + 2**b * (1 - 2 * bit_of(b))

    def at(ref, layer, off, size):
        return ref.at[layer, :, pl.ds(pl.multiple_of(off, LANE), size)]

    loads, grads = [], []
    for q in range(pipes):
        layer, base = q // groups, q % groups * width
        row = []
        for i, (src, dst) in enumerate(
            ((f_h, f_v), (s_h, s_v), (w_h, w_v), (a_h, a_v), (m_h, m_v))
        ):
            row.append(pltpu.make_async_copy(at(src, layer, base, width), at(dst, layer, base, width), in_sem.at[q, i]))
        row.append(
            pltpu.make_async_copy(at(g_h, layer, mine * cols + base, width), at(g_v, layer, base, width), in_sem.at[q, 5])
        )
        loads.append(row)
        row = []
        for s in range(1, n):
            peer = lax.rem(mine + s, n)
            row.append(
                pltpu.make_async_remote_copy(
                    src_ref=at(g_h, layer, peer * cols + base, width),
                    dst_ref=at(g_r.at[s - 1], layer, base, width),
                    send_sem=gs.at[q, s - 1],
                    recv_sem=gr.at[q, s - 1],
                    device_id={"fsdp": peer},
                    device_id_type=MESH,
                )
            )
        grads.append(row)

    barrier = pltpu.get_barrier_semaphore()
    for s in range(1, n):
        pl.semaphore_signal(barrier, inc=1, device_id={"fsdp": lax.rem(mine + s, n)}, device_id_type=MESH)
    for b in range(steps):
        pl.semaphore_signal(barrier, inc=1, device_id={"replica": partner(b)}, device_id_type=MESH)
    for row in loads:
        for copy in row:
            copy.start()
    pl.semaphore_wait(barrier, n - 1 + steps)
    for row in grads:
        for copy in row:
            copy.start()

    sent = []

    def outer(layer, off, size):
        def block(j, wide):
            c = pl.ds(pl.multiple_of(off + j, LANE), wide)
            moment_new, anchor_new = outer_update(tot[layer, :, c] * (1.0 / workers), m_v[layer, :, c], a_v[layer, :, c])
            moment_o[layer, :, c] = moment_new
            anchor_o[layer, :, c] = anchor_new
            d = pl.ds(pl.multiple_of(mine * cols + off + j, LANE), wide)
            fresh[layer, :, d] = anchor_new.astype(fresh.dtype)

        sweep(size, block)

    def pipe(q):
        layer, base = q // groups, q % groups * width
        slot = q % groups
        for copy in loads[q]:
            copy.wait()
        for copy in grads[q]:
            copy.wait_recv()
            sent.append(copy)

        def block(j, wide):
            c = pl.ds(pl.multiple_of(base + j, LANE), wide)
            gradient = g_v[layer, :, c].astype(jnp.float32)
            for s in range(n - 1):
                gradient = gradient + g_r[s, layer, :, c].astype(jnp.float32)
            first_new, second_new, pseudo = inner_update(
                w_v[layer, :, c], a_v[layer, :, c], f_v[layer, :, c], s_v[layer, :, c], gradient
            )
            first_o[layer, :, c] = first_new
            second_o[layer, :, c] = second_new
            acc[layer, :, c] = pseudo

        sweep(width, block)

        off, size = base, width
        offs = [off]
        for b in range(steps):
            if b < halvings:
                size //= 2
                give = off + (1 - bit_of(b)) * size
                off = off + bit_of(b) * size
                offs.append(off)
            else:
                give = off
            copy = pltpu.make_async_remote_copy(
                src_ref=at(acc, layer, give, size),
                dst_ref=at(parts[b], layer, slot * size, size),
                send_sem=rs.at[q, b],
                recv_sem=rr.at[q, b],
                device_id={"replica": partner(b)},
                device_id_type=MESH,
            )
            copy.start()
            yield
            if b < halvings:
                copy.wait_recv()
                sent.append(copy)
            else:
                copy.wait()
            into = tot if b == steps - 1 else acc

            def add(j, wide, b=b, off=off, size=size, into=into):
                c = pl.ds(pl.multiple_of(off + j, LANE), wide)
                d = pl.ds(pl.multiple_of(slot * size + j, LANE), wide)
                into[layer, :, c] = acc[layer, :, c] + parts[b][layer, :, d]

            sweep(size, add)

        for b in reversed(range(halvings)):
            copy = pltpu.make_async_remote_copy(
                src_ref=at(tot, layer, off, size),
                dst_ref=at(tot, layer, off, size),
                send_sem=ags.at[q, b],
                recv_sem=agr.at[q, b],
                device_id={"replica": partner(b)},
                device_id_type=MESH,
            )
            copy.start()
            sent.append(copy)
            if b == 0:
                outer(layer, off, size)
                fresh_out = []
                for s in range(1, n):
                    out = pltpu.make_async_remote_copy(
                        src_ref=at(fresh, layer, mine * cols + off, size),
                        dst_ref=at(fresh, layer, mine * cols + off, size),
                        send_sem=fs.at[q, s - 1],
                        recv_sem=fr.at[q, s - 1],
                        device_id={"fsdp": lax.rem(mine + s, n)},
                        device_id_type=MESH,
                    )
                    out.start()
                    sent.append(out)
                    fresh_out.append(out)
                half_off, half = off, size
            yield
            copy.wait_recv()
            off = offs[b]
            size *= 2
        outer(layer, base + (1 - bit_of(0)) * half, half)
        yield
        passed = []
        for s in range(1, n):
            fresh_out[s - 1].wait_recv()
            place = lax.rem(mine + n - s, n) * cols + half_off
            copy = pltpu.make_async_remote_copy(
                src_ref=at(fresh, layer, place, half),
                dst_ref=at(fresh, layer, place, half),
                send_sem=ws.at[q, s - 1],
                recv_sem=wr.at[q, s - 1],
                device_id={"replica": partner(0)},
                device_id_type=MESH,
            )
            copy.start()
            sent.append(copy)
            passed.append(copy)
        yield
        for copy in passed:
            copy.wait_recv()

    live = [pipe(q) for q in range(pipes)]
    turn = 0
    while any(p is not None for p in live):
        for q in range(pipes):
            if live[q] is not None and turn >= q * SKEW:
                try:
                    next(live[q])
                except StopIteration:
                    live[q] = None
        turn += 1
    for copy in sent:
        copy.wait_send()
    copy = pltpu.make_async_copy(fresh, fresh_o, out_sem)
    copy.start()
    copy.wait()


def put_out(*refs):
    count = len(refs) // 2
    sem = refs[-1]
    copies = [pltpu.make_async_copy(refs[i], refs[count + i], sem.at[i]) for i in range(count)]
    for copy in copies:
        copy.start()
    for copy in copies:
        copy.wait()


def solution(mesh):
    n, workers = mesh.shape["fsdp"], mesh.shape["replica"]

    def per_device(inner_weights, anchor, outer_moment, adam_first, adam_second, grad_parts):
        layers, rows, cols = anchor.shape
        pipes, width, halvings, steps = plan(cols, workers)
        shard, whole = (layers, rows, cols), (layers, rows, n * cols)
        f32, bf16 = jnp.float32, jnp.bfloat16
        parts = [
            pltpu.VMEM((layers, rows, pipes * (width >> min(b + 1, halvings))), f32) for b in range(steps)
        ]
        dma = pltpu.SemaphoreType.DMA
        total = layers * pipes
        outs = [jax.ShapeDtypeStruct(whole, bf16)] + [jax.ShapeDtypeStruct(shard, f32)] * 4
        limit = 67043328 - 2**18 - sum(o.size * o.dtype.itemsize for o in outs)
        results = pl.pallas_call(
            functools.partial(kernel, n, workers, pipes, width, halvings, steps),
            out_shape=[pltpu.VMEM(o.shape, o.dtype) for o in outs],
            in_specs=[pl.BlockSpec(memory_space=pltpu.HBM)] * 6,
            out_specs=[pl.BlockSpec(memory_space=pltpu.VMEM)] * 5,
            scratch_shapes=[pltpu.VMEM(shard, f32)] * 5
            + [pltpu.VMEM(shard, bf16), pltpu.VMEM((n - 1,) + shard, bf16)]
            + [pltpu.VMEM(shard, f32)] * 2
            + [pltpu.VMEM(whole, bf16)]
            + [dma((total, 6)), dma(())]
            + [dma((total, n - 1))] * 2
            + [dma((total, steps))] * 2
            + [dma((total, halvings))] * 2
            + [dma((total, n - 1))] * 4
            + parts,
            compiler_params=pltpu.CompilerParams(collective_id=0, has_side_effects=True, vmem_limit_bytes=limit),
        )(inner_weights[0], anchor, outer_moment, adam_first[0], adam_second[0], grad_parts[0, 0])
        fresh_weights, anchor_new, moment_new, first_new, second_new = pl.pallas_call(
            put_out,
            out_shape=outs,
            in_specs=[pl.BlockSpec(memory_space=pltpu.VMEM)] * 5,
            out_specs=[pl.BlockSpec(memory_space=pl.ANY)] * 5,
            scratch_shapes=[dma((5,))],
            compiler_params=pltpu.CompilerParams(vmem_limit_bytes=2**24),
        )(*results)
        return (fresh_weights, anchor_new, moment_new, first_new[None], second_new[None])

    in_specs = (
        P("replica", None, None, "fsdp"),
        P(None, None, "fsdp"),
        P(None, None, "fsdp"),
        P("replica", None, None, "fsdp"),
        P("replica", None, None, "fsdp"),
        P("replica", "fsdp", None, None, None),
    )
    out_specs = (
        P(),
        P(None, None, "fsdp"),
        P(None, None, "fsdp"),
        P("replica", None, None, "fsdp"),
        P("replica", None, None, "fsdp"),
    )
    return jax.shard_map(
        per_device, mesh=mesh, in_specs=in_specs, out_specs=out_specs, check_vma=False
    )
```

time: 55.1 us -> 42 us (0.76); the launches traced: 54.3 us -> 41.9 us
  local copies, waits for them, and re-layouts: 7.59 us -> 0 us
  Pallas kernels: 46.1 us -> 41.2 us
    unnamed x13 -> x0, local copies, waits for them, and re-layouts: 7.59 us -> none
    pallas_call x1, Pallas kernels: 46.1 us -> 39.1 us  [per_device(): pl.pallas_call(functools.partial(kernel, n, workers, pipes, width, halvin...]
    pallas_call x0 -> x1, Pallas kernels: none -> 2.12 us  [per_device(): pl.pallas_call(put_out, out_shape=outs, in_specs=[pl.BlockSpec(memory_spa...]
where the time goes in v2:
time: 42 us; the launch traced here: 41.9 us
  Pallas kernels  41.2 us (98%)
  between operations  0.64 us (2%)
    pallas_call x1, Pallas kernels, per_device(): pl.pallas_call(functools.partial(kernel, n, workers, pipes, width, halvin...  39.1 us
    pallas_call x1, Pallas kernels, per_device(): pl.pallas_call(put_out, out_shape=outs, in_specs=[pl.BlockSpec(memory_spa...  2.12 us

profile of v2, /device:TPU:0, one launch (start us, length us, event | category | flops | bytes accessed | tf_op | source)
XLA Modules:
  0.0 41.9 jit_solution(15374983084078714086)
XLA Ops:
  0.6 39.1 %shard_map.101 = (bf16[3,24,6144]{2,1,0:T(8,128)(2,1)S(1)}, f32[3,24,3072]{2,1,0:T(8,128)S(1)}, f32[3,24,3072]{2,1,0:T(8,128)S(1)}, f32[3,24,3072]{2,1,0:T(8,128)S(1)}, f32[3,24,3072]{2,1,0:T(8,128)S(1)}) custom-call(f32[3,24,3072]{2,1,0:T(8,128)} %bitcast.6, f32[3,24,3072]{2,1,0:T(8,128)} %refs_1_.1, f32[3,24,3072]{2,1,0:T(8,128)} %refs_2_.1, ...), custom_call_target="tpu_custom_call" | custom-call | tf_op jit(solution)/shard_map/pallas_call | solution.py:290
  39.8 2.1 %shard_map.102 = (bf16[3,24,6144]{2,1,0:T(8,128)(2,1)}, f32[3,24,3072]{2,1,0:T(8,128)}, f32[3,24,3072]{2,1,0:T(8,128)}, f32[3,24,3072]{2,1,0:T(8,128)}, f32[3,24,3072]{2,1,0:T(8,128)}) custom-call(bf16[3,24,6144]{2,1,0:T(8,128)(2,1)S(1)} %get-tuple-element.15.refs_0_, f32[3,24,3072]{2,1,0:T(8,128)S(1)} %get-tuple-element.16.refs_1_, ...), custom_call_target="tpu_custom_call" | custom-call | tf_op jit(solution)/shard_map/pallas_call | solution.py:307

commit v3 on v2

--- a/solution.py
+++ b/solution.py
@@ -115,10 +115,15 @@
         pl.semaphore_signal(barrier, inc=1, device_id={"fsdp": lax.rem(mine + s, n)}, device_id_type=MESH)
     for b in range(steps):
         pl.semaphore_signal(barrier, inc=1, device_id={"replica": partner(b)}, device_id_type=MESH)
+    quad = halvings >= 3
+    place4 = (me // 2) % 4
+    if quad:
+        far = partner(1) + partner(2) - me
+        pl.semaphore_signal(barrier, inc=1, device_id={"replica": far}, device_id_type=MESH)
     for row in loads:
         for copy in row:
             copy.start()
-    pl.semaphore_wait(barrier, n - 1 + steps)
+    pl.semaphore_wait(barrier, n - 1 + steps + (1 if quad else 0))
     for row in grads:
         for copy in row:
             copy.start()
@@ -162,6 +167,41 @@
         off, size = base, width
         offs = [off]
         for b in range(steps):
+            if quad and b == 1:
+                size //= 4
+                trio = []
+                for k in range(1, 4):
+                    other = (place4 + k) % 4
+                    copy = pltpu.make_async_remote_copy(
+                        src_ref=at(acc, layer, off + other * size, size),
+                        dst_ref=at(parts[1], layer, (slot * 3 + k - 1) * size, size),
+                        send_sem=rs.at[q, steps + k - 1],
+                        recv_sem=rr.at[q, steps + k - 1],
+                        device_id={"replica": me + 2 * (other - place4)},
+                        device_id_type=MESH,
+                    )
+                    copy.start()
+                    trio.append(copy)
+                offs.append(off)
+                off = off + place4 * size
+                offs.append(off)
+                yield
+                for copy in trio:
+                    copy.wait_recv()
+                    sent.append(copy)
+
+                def add4(j, wide, off=off, size=size):
+                    c = pl.ds(pl.multiple_of(off + j, LANE), wide)
+                    total = acc[layer, :, c]
+                    for k in range(3):
+                        d = pl.ds(pl.multiple_of((slot * 3 + k) * size + j, LANE), wide)
+                        total = total + parts[1][layer, :, d]
+                    (tot if steps == 3 else acc)[layer, :, c] = total
+
+                sweep(size, add4)
+                continue
+            if quad and b == 2:
+                continue
             if b < halvings:
                 size //= 2
                 give = off + (1 - bit_of(b)) * size
@@ -194,6 +234,29 @@
             sweep(size, add)
 
         for b in reversed(range(halvings)):
+            if quad and b == 2:
+                trio = []
+                for k in range(1, 4):
+                    other = (place4 + k) % 4
+                    copy = pltpu.make_async_remote_copy(
+                        src_ref=at(tot, layer, off, size),
+                        dst_ref=at(tot, layer, off, size),
+                        send_sem=ags.at[q, halvings + k - 1],
+                        recv_sem=agr.at[q, halvings + k - 1],
+                        device_id={"replica": me + 2 * (other - place4)},
+                        device_id_type=MESH,
+                    )
+                    copy.start()
+                    sent.append(copy)
+                    trio.append(copy)
+                yield
+                for copy in trio:
+                    copy.wait_recv()
+                off = offs[1]
+                size *= 4
+                continue
+            if quad and b == 1:
+                continue
             copy = pltpu.make_async_remote_copy(
                 src_ref=at(tot, layer, off, size),
                 dst_ref=at(tot, layer, off, size),
@@ -283,6 +346,8 @@
         parts = [
             pltpu.VMEM((layers, rows, pipes * (width >> min(b + 1, halvings))), f32) for b in range(steps)
         ]
+        if halvings >= 3:
+            parts[1] = pltpu.VMEM((layers, rows, pipes * 3 * (width >> 3)), f32)
         dma = pltpu.SemaphoreType.DMA
         total = layers * pipes
         outs = [jax.ShapeDtypeStruct(whole, bf16)] + [jax.ShapeDtypeStruct(shard, f32)] * 4
@@ -298,8 +363,8 @@
             + [pltpu.VMEM(whole, bf16)]
             + [dma((total, 6)), dma(())]
             + [dma((total, n - 1))] * 2
-            + [dma((total, steps))] * 2
-            + [dma((total, halvings))] * 2
+            + [dma((total, steps + 3))] * 2
+            + [dma((total, halvings + 3))] * 2
             + [dma((total, n - 1))] * 4
             + parts,
             compiler_params=pltpu.CompilerParams(collective_id=0, has_side_effects=True, vmem_limit_bytes=limit),

time: 42 us -> 41.3 us (0.983)
  Pallas kernels: 41.2 us -> 40.5 us
    pallas_call x1, Pallas kernels: 39.1 us -> 38.4 us  [per_device(): pl.pallas_call(functools.partial(kernel, n, workers, pipes, width, halvin...]
where the time goes in v3:
time: 41.3 us; the launch traced here: 41.1 us
  Pallas kernels  40.5 us (98%)
  between operations  0.64 us (2%)
    pallas_call x1, Pallas kernels, per_device(): pl.pallas_call(functools.partial(kernel, n, workers, pipes, width, halvin...  38.4 us
    pallas_call x1, Pallas kernels, per_device(): pl.pallas_call(put_out, out_shape=outs, in_specs=[pl.BlockSpec(memory_spa...  2.12 us

profile of v3, /device:TPU:0, one launch (start us, length us, event | category | flops | bytes accessed | tf_op | source)
XLA Modules:
  0.0 41.1 jit_solution(10195729886814613081)
XLA Ops:
  0.6 38.4 %shard_map.101 = (bf16[3,24,6144]{2,1,0:T(8,128)(2,1)S(1)}, f32[3,24,3072]{2,1,0:T(8,128)S(1)}, f32[3,24,3072]{2,1,0:T(8,128)S(1)}, f32[3,24,3072]{2,1,0:T(8,128)S(1)}, f32[3,24,3072]{2,1,0:T(8,128)S(1)}) custom-call(f32[3,24,3072]{2,1,0:T(8,128)} %bitcast.6, f32[3,24,3072]{2,1,0:T(8,128)} %refs_1_.1, f32[3,24,3072]{2,1,0:T(8,128)} %refs_2_.1, ...), custom_call_target="tpu_custom_call" | custom-call | tf_op jit(solution)/shard_map/pallas_call | solution.py:355
  39.0 2.1 %shard_map.102 = (bf16[3,24,6144]{2,1,0:T(8,128)(2,1)}, f32[3,24,3072]{2,1,0:T(8,128)}, f32[3,24,3072]{2,1,0:T(8,128)}, f32[3,24,3072]{2,1,0:T(8,128)}, f32[3,24,3072]{2,1,0:T(8,128)}) custom-call(bf16[3,24,6144]{2,1,0:T(8,128)(2,1)S(1)} %get-tuple-element.15.refs_0_, f32[3,24,3072]{2,1,0:T(8,128)S(1)} %get-tuple-element.16.refs_1_, ...), custom_call_target="tpu_custom_call" | custom-call | tf_op jit(solution)/shard_map/pallas_call | solution.py:372
